TPU v7x, 32 devices: a whole 2x2x4 slice. The times are simulated.
32 devices in a mesh: rep: 4 (over y, x), shard: 8 (over z, core).
Axes of the slice: x: 2, y: 2, z: 4, core: 2. Of those that a mesh axis runs over, the one named last changes fastest.
Arguments:
- tokens: bfloat16 [16, 2048, 768], P('shard', 'rep'), may hold values from -6 to 6
- segment_ids: int32 [16, 2048], P('shard'), may hold values from 0 to 7, never falling along the last dimension, each value on 1 to 1024 neighbouring positions
- cotangent: bfloat16 [16, 2048, 768], P('shard', 'rep'), may hold values from -6 to 6
- query_weight: bfloat16 [768, 768], P('shard'), may hold values from -0.3125 to 0.3125
- key_weight: bfloat16 [768, 768], P('shard'), may hold values from -0.3125 to 0.3125
- value_weight: bfloat16 [768, 768], P('shard'), may hold values from -0.21875 to 0.21875
- output_weight: bfloat16 [768, 768], P('shard'), may hold values from -1.5 to 1.5
- expand_weight: bfloat16 [768, 3072], P('shard'), may hold values from -0.21875 to 0.21875
- reduce_weight: bfloat16 [3072, 768], P('shard'), may hold values from -0.109375 to 0.109375
- query_bias: bfloat16 [768], P('shard'), may hold values from -1.5 to 1.5
- value_bias: bfloat16 [768], P('shard'), may hold values from -0.5 to 0.5
- output_bias: bfloat16 [768], P('shard'), may hold values from -1.5 to 1.5
- expand_bias: bfloat16 [3072], P('shard'), may hold values from -1.5 to 1.5
- reduce_bias: bfloat16 [768], P('shard'), may hold values from -1.5 to 1.5
- first_gain: bfloat16 [768], P('shard'), may hold values from 0.099609375 to 1.8984375
- first_shift: bfloat16 [768], P('shard'), may hold values from -1.5 to 1.5
- second_gain: bfloat16 [768], P('shard'), may hold values from 0.099609375 to 1.8984375
- second_shift: bfloat16 [768], P('shard'), may hold values from -1.5 to 1.5
Outputs:
- layer_output: bfloat16 [16, 2048, 768], P('shard', 'rep')
- tokens_gradient: bfloat16 [16, 2048, 768], P('shard', 'rep')
- query_weight_gradient: float32 [768, 768], P('shard')
- key_weight_gradient: float32 [768, 768], P('shard')
- value_weight_gradient: float32 [768, 768], P('shard')
- output_weight_gradient: float32 [768, 768], P('shard')
- expand_weight_gradient: float32 [768, 3072], P('shard')
- reduce_weight_gradient: float32 [3072, 768], P('shard')
- query_bias_gradient: float32 [768], P('shard')
- value_bias_gradient: float32 [768], P('shard')
- output_bias_gradient: float32 [768], P('shard')
- expand_bias_gradient: float32 [3072], P('shard')
- reduce_bias_gradient: float32 [768], P('shard')
- first_gain_gradient: float32 [768], P('shard')
- first_shift_gradient: float32 [768], P('shard')
- second_gain_gradient: float32 [768], P('shard')
- second_shift_gradient: float32 [768], P('shard')
Inputs may be any that keep to these rules, and one draw needn't show every extreme that they name: `segment_ids`: within each sequence the ids never fall; each document holds 1 to 1024 positions and some document of each sequence exactly 1024.
All inputs are finite; a program needn't handle non-finite values.
Results may differ from a plain program's by a relative error of at most 0.017.
The roundings to bfloat16 on the way count: a program that leaves them out, or rounds other values in their place, can miss the bound.
Values may be sent and summed in bfloat16 or wider, within the bound.
A program may use at most 448 MiB of HBM per device.

v0:
```python
from functools import partial
import jax
import jax.numpy as jnp
from jax import lax
from jax.sharding import PartitionSpec as P

HEAD_DIM = 64
masked_value = -1e30
norm_eps = 1e-05


def as_sent(array):
    return jax.tree.map(lambda a: a.astype(jnp.bfloat16) if a.dtype == jnp.float32 else a, array)


def norm_rows(values, gain, shift):
    centre = values - jnp.mean(values, axis=-1, keepdims=True)
    spread = jnp.mean(centre * centre, axis=-1, keepdims=True)
    return centre * lax.rsqrt(spread + norm_eps) * gain + shift


def dense(left, right):
    return jnp.dot(left, right, preferred_element_type=jnp.float32)


def dense_left(left, right):
    return lax.dot_general(
        left, right, (((0,), (0,)), ((), ())), preferred_element_type=jnp.float32
    )


def dense_right(left, right):
    return lax.dot_general(
        left, right, (((1,), (1,)), ((), ())), preferred_element_type=jnp.float32
    )


def column_sum(values):
    return jnp.sum(values.astype(jnp.float32), axis=0)


def unpack(weights):
    matrices = weights[:6]
    vectors = tuple((member.astype(jnp.float32) for member in weights[6:]))
    return (matrices, vectors)


def block_scores(query_block, key_heads, allowed_blocks, block_rows):
    factor = query_block.shape[2] ** (-0.5)
    pieces = []
    for number in range(len(allowed_blocks)):
        allowed = allowed_blocks[number]
        key_block = key_heads[number * block_rows : (number + 1) * block_rows]
        product = partial(
            jnp.einsum, "qhd,khd->hqk", query_block, key_block, preferred_element_type=jnp.float32
        )
        unmasked = product()
        pieces.append(jnp.where(allowed[None, :, :], unmasked * factor, masked_value))
    return jnp.concatenate(pieces, axis=2)


def allowed_for(query_segments, segment_keys, block_rows, key_count):
    return [
        query_segments[:, None]
        == segment_keys[number * block_rows : (number + 1) * block_rows][None, :]
        for number in range(key_count)
    ]


def attend_forward(query_heads, key_heads, value_heads, segment_query, segment_whole):
    local_rows = query_heads.shape[0]
    block_rows = min(512, local_rows)
    key_count = key_heads.shape[0] // block_rows
    allowed_blocks = allowed_for(segment_query, segment_whole, block_rows, key_count)
    scores = block_scores(query_heads, key_heads, allowed_blocks, block_rows)
    largest = jnp.max(scores, axis=2, keepdims=True)
    exponent = jnp.exp(scores - largest)
    row_total = jnp.sum(exponent, axis=2, keepdims=True)
    chances = (exponent / row_total).astype(jnp.bfloat16)
    logsums = [largest[:, :, 0] + jnp.log(row_total[:, :, 0])]
    mixture = jnp.zeros(query_heads.shape, jnp.float32)
    for number in range(key_count):
        chance_slice = chances[:, :, number * block_rows : (number + 1) * block_rows]
        value_block = value_heads[number * block_rows : (number + 1) * block_rows]
        product = partial(
            jnp.einsum,
            "hqk,khd->qhd",
            chance_slice,
            value_block,
            preferred_element_type=jnp.float32,
        )
        mixture = mixture + product()
    mixtures = [mixture]
    return (jnp.concatenate(mixtures, axis=0), jnp.concatenate(logsums, axis=1))


def attend_backward(
    query_heads,
    key_heads,
    value_heads,
    segment_query,
    segment_keys,
    logsums,
    grad_heads,
    block_rows,
):
    query_rows, head_count, head_width = query_heads.shape
    key_count = key_heads.shape[0] // block_rows
    factor = head_width ** (-0.5)
    block_shape = (block_rows, head_count, head_width)
    key_grads = [jnp.zeros(block_shape, jnp.float32) for number in range(key_count)]
    value_grads = [jnp.zeros(block_shape, jnp.float32) for number in range(key_count)]
    allowed_blocks = allowed_for(segment_query, segment_keys, block_rows, key_count)
    scores = block_scores(query_heads, key_heads, allowed_blocks, block_rows)
    chances = jnp.exp(scores - logsums[:, 0:block_rows, None])
    chance_low = chances.astype(jnp.bfloat16)
    pieces = []
    for number in range(key_count):
        value_block = value_heads[number * block_rows : (number + 1) * block_rows]
        product = partial(
            jnp.einsum, "qhd,khd->hqk", grad_heads, value_block, preferred_element_type=jnp.float32
        )
        pieces.append(product())
    grad_chances = jnp.concatenate(pieces, axis=2)
    centre = jnp.sum(chances * grad_chances, axis=2, keepdims=True)
    centres = [centre[:, :, 0]]
    grad_scores = (chances * (grad_chances - centre)).astype(jnp.bfloat16)
    query_grad = jnp.zeros(block_shape, jnp.float32)
    for number in range(key_count):
        key_block = key_heads[number * block_rows : (number + 1) * block_rows]
        score_slice = grad_scores[:, :, number * block_rows : (number + 1) * block_rows]
        chance_slice = chance_low[:, :, number * block_rows : (number + 1) * block_rows]
        query_grad = (
            query_grad
            + partial(
                jnp.einsum,
                "hqk,khd->qhd",
                score_slice,
                key_block,
                preferred_element_type=jnp.float32,
            )()
        )
        key_grads[number] = (
            key_grads[number]
            + partial(
                jnp.einsum,
                "hqk,qhd->khd",
                score_slice,
                query_heads,
                preferred_element_type=jnp.float32,
            )()
        )
        value_grads[number] = (
            value_grads[number]
            + partial(
                jnp.einsum,
                "hqk,qhd->khd",
                chance_slice,
                grad_heads,
                preferred_element_type=jnp.float32,
            )()
        )
    query_grads = [query_grad * factor]
    key_whole = jnp.concatenate(key_grads, axis=0) * factor
    return (
        jnp.concatenate(query_grads, axis=0),
        key_whole,
        jnp.concatenate(value_grads, axis=0),
        jnp.concatenate(centres, axis=1),
    )


def local(
    tokens,
    segment_ids,
    cotangent,
    query_weight,
    key_weight,
    value_weight,
    output_weight,
    expand_weight,
    reduce_weight,
    query_bias,
    value_bias,
    output_bias,
    expand_bias,
    reduce_bias,
    first_gain,
    first_shift,
    second_gain,
    second_shift,
):
    shards = (
        query_weight,
        key_weight,
        value_weight,
        output_weight,
        expand_weight,
        reduce_weight,
        query_bias,
        value_bias,
        output_bias,
        expand_bias,
        reduce_bias,
        first_gain,
        first_shift,
        second_gain,
        second_shift,
    )
    micro_count = tokens.shape[0]
    local_rows = tokens.shape[1]
    model_width = tokens.shape[2]
    head_count = model_width // HEAD_DIM
    block_rows = min(512, local_rows)
    offset = lax.axis_index("rep") * local_rows
    totals = tuple(
        (
            jnp.zeros((lax.axis_size("shard") * member.shape[0],) + member.shape[1:], jnp.float32)
            for member in shards
        )
    )
    outputs = []
    input_grads = []

    def heads_of(array):
        return array.reshape(array.shape[0], head_count, HEAD_DIM)

    for micro_index in range(micro_count):
        weights_now = (
            lax.all_gather(shards[0], "shard", axis=0, tiled=True),
            lax.all_gather(shards[1], "shard", axis=0, tiled=True),
            lax.all_gather(shards[2], "shard", axis=0, tiled=True),
            lax.all_gather(shards[3], "shard", axis=0, tiled=True),
            lax.all_gather(shards[4], "shard", axis=0, tiled=True),
            lax.all_gather(shards[5], "shard", axis=0, tiled=True),
            lax.all_gather(shards[6], "shard", axis=0, tiled=True),
            lax.all_gather(shards[7], "shard", axis=0, tiled=True),
            lax.all_gather(shards[8], "shard", axis=0, tiled=True),
            lax.all_gather(shards[9], "shard", axis=0, tiled=True),
            lax.all_gather(shards[10], "shard", axis=0, tiled=True),
            lax.all_gather(shards[11], "shard", axis=0, tiled=True),
            lax.all_gather(shards[12], "shard", axis=0, tiled=True),
            lax.all_gather(shards[13], "shard", axis=0, tiled=True),
            lax.all_gather(shards[14], "shard", axis=0, tiled=True),
        )
        matrices, vectors = unpack(weights_now)
        query_matrix, key_matrix, value_matrix, output_matrix, expand_matrix, reduce_matrix = (
            matrices
        )
        (
            query_vector,
            value_vector,
            output_vector,
            expand_vector,
            reduce_vector,
            first_gain_vec,
            first_shift_vec,
            second_gain_vec,
            second_shift_vec,
        ) = vectors
        inputs_now = tokens[micro_index]
        segment_whole = segment_ids[micro_index]
        segment_query = lax.dynamic_slice_in_dim(segment_whole, offset, local_rows)
        queries = (dense(inputs_now, query_matrix) + query_vector).astype(jnp.bfloat16)
        keys_local = dense(inputs_now, key_matrix).astype(jnp.bfloat16)
        values_local = (dense(inputs_now, value_matrix) + value_vector).astype(jnp.bfloat16)
        keys_whole, values_whole = (
            lax.all_gather(keys_local, "rep", axis=0, tiled=True),
            lax.all_gather(values_local, "rep", axis=0, tiled=True),
        )
        mixture, logsums = attend_forward(
            heads_of(queries),
            heads_of(keys_whole),
            heads_of(values_whole),
            segment_query,
            segment_whole,
        )
        attended = mixture.reshape(local_rows, model_width).astype(jnp.bfloat16)
        branch = dense(attended, output_matrix) + output_vector
        first, first_back = jax.vjp(
            norm_rows, inputs_now.astype(jnp.float32) + branch, first_gain_vec, first_shift_vec
        )
        first_low = first.astype(jnp.bfloat16)
        expanded = dense(first_low, expand_matrix) + expand_vector
        activated, gelu_back = jax.vjp(jax.nn.gelu, expanded)
        activated_low = activated.astype(jnp.bfloat16)
        reduced = dense(activated_low, reduce_matrix) + reduce_vector
        result, second_back = jax.vjp(norm_rows, first + reduced, second_gain_vec, second_shift_vec)
        outputs.append(result.astype(jnp.bfloat16))
        weights_now = (
            lax.all_gather(shards[0], "shard", axis=0, tiled=True),
            lax.all_gather(shards[1], "shard", axis=0, tiled=True),
            lax.all_gather(shards[2], "shard", axis=0, tiled=True),
            lax.all_gather(shards[3], "shard", axis=0, tiled=True),
            lax.all_gather(shards[4], "shard", axis=0, tiled=True),
            lax.all_gather(shards[5], "shard", axis=0, tiled=True),
            lax.all_gather(shards[6], "shard", axis=0, tiled=True),
            lax.all_gather(shards[7], "shard", axis=0, tiled=True),
            lax.all_gather(shards[8], "shard", axis=0, tiled=True),
            lax.all_gather(shards[9], "shard", axis=0, tiled=True),
            lax.all_gather(shards[10], "shard", axis=0, tiled=True),
            lax.all_gather(shards[11], "shard", axis=0, tiled=True),
            lax.all_gather(shards[12], "shard", axis=0, tiled=True),
            lax.all_gather(shards[13], "shard", axis=0, tiled=True),
            lax.all_gather(shards[14], "shard", axis=0, tiled=True),
        )
        matrices, vectors = unpack(weights_now)
        query_matrix, key_matrix, value_matrix, output_matrix, expand_matrix, reduce_matrix = (
            matrices
        )
        grad_second, grad_second_gain, grad_second_shift = second_back(
            cotangent[micro_index].astype(jnp.float32)
        )
        grad_reduced = grad_second.astype(jnp.bfloat16)
        reduce_matrix_grad = dense_left(activated_low, grad_reduced)
        (grad_expanded_full,) = gelu_back(dense_right(grad_reduced, reduce_matrix))
        grad_expanded = grad_expanded_full.astype(jnp.bfloat16)
        expand_matrix_grad = dense_left(first_low, grad_expanded)
        grad_first = grad_second + dense_right(grad_expanded, expand_matrix)
        grad_residual, grad_first_gain, grad_first_shift = first_back(grad_first)
        grad_branch = grad_residual.astype(jnp.bfloat16)
        output_matrix_grad = dense_left(attended, grad_branch)
        grad_attended = dense_right(grad_branch, output_matrix).astype(jnp.bfloat16)
        query_side = attend_backward(
            heads_of(queries),
            heads_of(keys_whole),
            heads_of(values_whole),
            segment_query,
            segment_whole,
            logsums,
            heads_of(grad_attended),
            block_rows,
        )
        grad_query_heads = query_side[0]
        key_terms = query_side[1]
        value_terms = query_side[2]
        sequence_rows = key_terms.shape[0]
        grad_keys_full, grad_values_full = (
            lax.psum_scatter(
                key_terms.reshape(sequence_rows, model_width),
                "rep",
                scatter_dimension=0,
                tiled=True,
            ),
            lax.psum_scatter(
                value_terms.reshape(sequence_rows, model_width),
                "rep",
                scatter_dimension=0,
                tiled=True,
            ),
        )
        grad_queries = grad_query_heads.reshape(local_rows, model_width).astype(jnp.bfloat16)
        grad_keys = grad_keys_full.astype(jnp.bfloat16)
        grad_values = grad_values_full.astype(jnp.bfloat16)
        grad_inputs = (
            grad_residual
            + dense_right(grad_queries, query_matrix)
            + dense_right(grad_keys, key_matrix)
            + dense_right(grad_values, value_matrix)
        )
        input_grads.append(grad_inputs.astype(jnp.bfloat16))
        changes = (
            dense_left(inputs_now, grad_queries),
            dense_left(inputs_now, grad_keys),
            dense_left(inputs_now, grad_values),
            output_matrix_grad,
            expand_matrix_grad,
            reduce_matrix_grad,
            column_sum(grad_queries),
            column_sum(grad_values),
            column_sum(grad_branch),
            column_sum(grad_expanded),
            column_sum(grad_reduced),
            grad_first_gain,
            grad_first_shift,
            grad_second_gain,
            grad_second_shift,
        )
        totals = tuple((total + change for total, change in zip(totals, changes)))
    summed = lax.psum_scatter(totals, "shard", scatter_dimension=0, tiled=True)
    final = jax.tree.map(lambda part: part.astype(jnp.float32), lax.psum(as_sent(summed), "rep"))
    return (jnp.stack(outputs), jnp.stack(input_grads)) + tuple(final)


def solution(mesh):
    in_specs = (
        P("shard", "rep", None),
        P("shard", None),
        P("shard", "rep", None),
        P("shard", None),
        P("shard", None),
        P("shard", None),
        P("shard", None),
        P("shard", None),
        P("shard", None),
        P("shard"),
        P("shard"),
        P("shard"),
        P("shard"),
        P("shard"),
        P("shard"),
        P("shard"),
        P("shard"),
        P("shard"),
    )
    out_specs = (
        P("shard", "rep", None),
        P("shard", "rep", None),
        P("shard", None),
        P("shard", None),
        P("shard", None),
        P("shard", None),
        P("shard", None),
        P("shard", None),
        P("shard"),
        P("shard"),
        P("shard"),
        P("shard"),
        P("shard"),
        P("shard"),
        P("shard"),
        P("shard"),
        P("shard"),
    )
    return jax.shard_map(local, mesh=mesh, in_specs=in_specs, out_specs=out_specs, check_vma=False)
```

profile of v0, /device:TPU:0, one launch (start us, length us, event | category | flops | bytes accessed | tf_op | source)
XLA Modules:
  0.0 1376.7 jit_solution(11595395446563708483)
XLA Ops:
  18.2 30.6 %all-reduce.18 = (bf16[768]{0:T(1024)(128)(2,1)S(1)}, bf16[768]{0:T(1024)(128)(2,1)S(1)}, bf16[768]{0:T(1024)(128)(2,1)S(1)}, bf16[768]{0:T(1024)(128)(2,1)S(1)}...) all-reduce(bf16[768]{0:T(1024)(128)(2,1)S(1)} %dynamic-update-slice, ...), channel_id=1, replica_groups=mesh['rep'=4,'shard'=8] {'shard'}, use_global_device_ids=true, to_apply=%add | all-reduce | flops 6144 | bytes 24576
  70.3 12.7 all-gather
  93.8 35.4 %all-gather.28.cloned.1.call-done = bf16[2048,768]{1,0:T(8,128)(2,1)} async-done(((bf16[512,768]{1,0:T(8,128)(2,1)}), bf16[2048,768]{1,0:T(8,128)(2,1)}) %all-gather.28.cloned.1.call-update) | async-done | bytes 3145744 | tf_op jit(solution)/shard_map/all_gather | solution.py:269
  135.1 40.4 %all-gather.14.cloned.1.call-done = bf16[2048,768]{1,0:T(8,128)(2,1)} async-done(((bf16[512,768]{1,0:T(8,128)(2,1)}), bf16[2048,768]{1,0:T(8,128)(2,1)}) %all-gather.14.cloned.1.call-update) | async-done | bytes 3145744 | tf_op jit(solution)/shard_map/all_gather | solution.py:269
  195.3 25.8 %all-gather.30.cloned.1.call-done = bf16[2048,768]{1,0:T(8,128)(2,1)} async-done(((bf16[512,768]{1,0:T(8,128)(2,1)}), bf16[2048,768]{1,0:T(8,128)(2,1)}) %all-gather.30.cloned.1.call-update) | async-done | bytes 3145744 | tf_op jit(solution)/shard_map/all_gather | solution.py:268
  234.0 33.0 %all-gather.20.cloned.1.call-done = bf16[2048,768]{1,0:T(8,128)(2,1)} async-done(((bf16[512,768]{1,0:T(8,128)(2,1)}), bf16[2048,768]{1,0:T(8,128)(2,1)}) %all-gather.20.cloned.1.call-update) | async-done | bytes 3145744 | tf_op jit(solution)/shard_map/all_gather | solution.py:268
  308.6 17.5 %fusion.5 = f32[12,512]{1,0:T(8,128)S(1)} fusion(f32[12,512]{1,0:T(8,128)S(1)} %maximum_maximum_fusion, f32[12,512,512]{1,2,0:T(8,128)} %get-tuple-element.199, f32[12,512,512]{1,2,0:T(8,128)} %get-tuple-element.201, f32[12,512,512]{1,2,0:T(8,128)} %get-tuple-element.205, f32[12,512,512]{1,2,0:T(8,128)} %get-tuple-element.203), kind=kLoop, calls=%fused_computation.19 | loop fusion | flops 62908416 | bytes 50380800 | tf_op jit(solution)/shard_map/reduce_sum | solution.py:78
  354.2 17.3 %fusion.4 = f32[12,512]{1,0:T(8,128)S(1)} fusion(f32[12,512]{1,0:T(8,128)S(1)} %maximum_maximum_fusion.1, f32[12,512,512]{1,2,0:T(8,128)} %get-tuple-element.187, f32[12,512,512]{1,2,0:T(8,128)} %get-tuple-element.189, f32[12,512,512]{1,2,0:T(8,128)} %get-tuple-element.193, f32[12,512,512]{1,2,0:T(8,128)} %get-tuple-element.191), kind=kLoop, calls=%fused_computation.18 | loop fusion | flops 62908416 | bytes 50380800 | tf_op jit(solution)/shard_map/reduce_sum | solution.py:78
  371.5 39.4 %fusion.6 = (bf16[12,512,2048]{1,2,0:T(8,128)(2,1)}, bf16[12,512,2048]{1,2,0:T(8,128)(2,1)}) fusion(f32[12,512]{1,0:T(8,128)S(1)} %log_add_fusion.1, f32[12,512,512]{1,2,0:T(8,128)} %get-tuple-element.187, f32[12,512,512]{1,2,0:T(8,128)} %get-tuple-element.189, f32[12,512,512]{1,2,0:T(8,128)} %get-tuple-element.193, f32[12,512,512]{1,2,0:T(8,128)} %get-tuple-element.191, ...), kind=kLoop, calls=%fused_computation.20 | loop fusion | flops 100663296 | bytes 100737024 | tf_op jit(solution)/shard_map/convert_element_type | solution.py:116
  431.1 39.2 %fusion.9 = (bf16[12,512,2048]{1,2,0:T(8,128)(2,1)}, bf16[12,512,2048]{1,2,0:T(8,128)(2,1)}) fusion(f32[12,512]{1,0:T(8,128)S(1)} %log_add_fusion, f32[12,512,512]{1,2,0:T(8,128)} %get-tuple-element.199, f32[12,512,512]{1,2,0:T(8,128)} %get-tuple-element.201, f32[12,512,512]{1,2,0:T(8,128)} %get-tuple-element.205, f32[12,512,512]{1,2,0:T(8,128)} %get-tuple-element.203, ...), kind=kLoop, calls=%fused_computation.21 | loop fusion | flops 100663296 | bytes 100737024 | tf_op jit(solution)/shard_map/convert_element_type | solution.py:116
  488.1 8.4 fusion.190
  522.8 18.1 %convert_reduce_fusion.1 = (f32[3072]{0:T(1024)}, bf16[512,3072]{1,0:T(8,128)(2,1)}, f32[3072]{0:T(1024)}, bf16[512,3072]{1,0:T(8,128)(2,1)S(1)}) fusion(f32[512,3072]{1,0:T(8,128)} %fusion.190, f32[3072]{0:T(1024)S(1)} %bitcast.362, f32[512,3072]{1,0:T(8,128)} %fusion.223, f32[512,3072]{1,0:T(8,128)} %copy-done.124, ...), kind=kOutput, calls=%fused_computation.87 | convolution fusion | flops 2488264704 | bytes 30707712 | tf_op jit(solution)/shard_map/dot_general | solution.py:33
  629.2 76.6 %multiply_convert_fusion.1 = bf16[12,512,2048]{1,2,0:T(8,128)(2,1)} fusion(f32[12,512,512]{1,2,0:T(8,128)} %fusion.221, f32[12,512,512]{1,2,0:T(8,128)} %fusion.220, f32[12,512,512]{1,2,0:T(8,128)} %fusion.219, f32[12,512,512]{1,2,0:T(8,128)} %fusion.218, f32[12,512]{1,0:T(8,128)S(1)} %copy-done.86, f32[12,512,512]{1,2,0:T(8,128)} %get-tuple-element.187, ...), kind=kOutput, calls=%fused_computation.10 | output fusion | flops 226500608 | bytes 125853696 | tf_op jit(solution)/shard_map/sub | solution.py:127
  754.2 87.6 %multiply_convert_fusion = bf16[12,512,2048]{1,2,0:T(8,128)(2,1)} fusion(f32[12,512,512]{1,2,0:T(8,128)} %fusion.227, f32[12,512,512]{1,2,0:T(8,128)} %fusion.226, f32[12,512,512]{1,2,0:T(8,128)} %fusion.225, f32[12,512,512]{1,2,0:T(8,128)} %fusion.224, f32[12,512]{1,0:T(8,128)S(1)} %copy-done.84, f32[12,512,512]{1,2,0:T(8,128)} %get-tuple-element.199, ...), kind=kOutput, calls=%fused_computation.6 | output fusion | flops 226500608 | bytes 125853696 | tf_op jit(solution)/shard_map/sub | solution.py:127
  921.2 13.1 reduce-scatter.21.cloned.1.call-done
  948.2 10.2 convolution_add_fusion
  983.1 27.4 %reduce-scatter.31.cloned.1.call-done = f32[96,768]{1,0:T(8,128)} async-done(((f32[768,768]{1,0:T(8,128)}), f32[96,768]{1,0:T(8,128)}) %reduce-scatter.31.cloned.1.call-update) | async-done | bytes 294928
  1012.4 35.7 %reduce-scatter.35.cloned.1.call-done = f32[96,768]{1,0:T(8,128)} async-done(((f32[768,768]{1,0:T(8,128)}), f32[96,768]{1,0:T(8,128)}) %reduce-scatter.35.cloned.1.call-update) | async-done | bytes 294928
  1049.9 35.8 %reduce-scatter.33.cloned.1.call-done = f32[96,768]{1,0:T(8,128)} async-done(((f32[768,768]{1,0:T(8,128)}), f32[96,768]{1,0:T(8,128)}) %reduce-scatter.33.cloned.1.call-update) | async-done | bytes 294928
  1087.5 99.2 %reduce-scatter.29.cloned.1.call-done = f32[384,768]{1,0:T(8,128)} async-done(((f32[3072,768]{1,0:T(8,128)}), f32[384,768]{1,0:T(8,128)}) %reduce-scatter.29.cloned.1.call-update) | async-done | bytes 1179664 | tf_op jit(solution)/shard_map/reduce_scatter | solution.py:380
  1188.9 97.9 %reduce-scatter.27.cloned.1.call-done = f32[96,3072]{1,0:T(8,128)} async-done(((f32[768,3072]{1,0:T(8,128)}), f32[96,3072]{1,0:T(8,128)}) %reduce-scatter.27.cloned.1.call-update) | async-done | bytes 1179664 | tf_op jit(solution)/shard_map/reduce_scatter | solution.py:380
  1289.2 26.4 %all-reduce.17 = (bf16[768]{0:T(1024)(128)(2,1)S(1)}, bf16[768]{0:T(1024)(128)(2,1)S(1)}, bf16[768]{0:T(1024)(128)(2,1)S(1)}, bf16[3072]{0:T(1024)(128)(2,1)S(1)...) all-reduce(f32[768]{0:T(1024)S(1)} %add.445, ...), channel_id=12, replica_groups=mesh['rep'=4,'shard'=8] {'shard'}, use_global_device_ids=true, to_apply=%region_46.47.clone | all-reduce | flops 9216 | bytes 55296
  1316.3 10.0 all-reduce.19
  1340.1 18.0 %all-reduce.23.cloned.1.call-done = (bf16[96,768]{0,1:T(8,128)(2,1)}, bf16[96,768]{0,1:T(8,128)(2,1)}, bf16[96,768]{0,1:T(8,128)(2,1)}, bf16[96,768]{1,0:T(8,128...) async-done(((bf16[96,768]{0,1:T(8,128)(2,1)}, bf16[96,768]{0,1:T(8,128)(2,1)}, bf16[96,768]{0,1:T(8,128)(2,1)}, bf16[96,768]{1,0:T(8,128)(2,1)}, ...) | async-done | bytes 1769488 | tf_op jit(solution)/shard_map/psum | solution.py:381
  (542 shorter events, 501.9 us)
Async XLA Ops:
  7.2 41.5 %all-gather.12.cloned.1.call-start = ((), (), s32[]{:S(2)}) async-start(), calls=%async_computation.10 | async-start | bytes 1327104 | tf_op jit(solution)/shard_map/all_gather | solution.py:232
  7.9 51.3 %all-gather.18.cloned.1.call-start = ((), (), s32[]{:S(2)}) async-start(), calls=%async_computation.13 | async-start | bytes 1327104 | tf_op jit(solution)/shard_map/all_gather | solution.py:231
  8.7 78.0 %all-gather.16.cloned.1.call-start = ((), (), s32[]{:S(2)}) async-start(), calls=%async_computation.12 | async-start | bytes 1327104 | tf_op jit(solution)/shard_map/all_gather | solution.py:230
  9.4 119.8 %all-gather.28.cloned.1.call-start = ((), (), s32[]{:S(2)}) async-start(), calls=%async_computation.18 | async-start | bytes 3932160 | tf_op jit(solution)/shard_map/all_gather | solution.py:269
  52.1 123.4 %all-gather.14.cloned.1.call-start = ((), (), s32[]{:S(2)}) async-start(), calls=%async_computation.11 | async-start | bytes 3932160 | tf_op jit(solution)/shard_map/all_gather | solution.py:269
  53.8 167.3 %all-gather.30.cloned.1.call-start = ((), (), s32[]{:S(2)}) async-start(), calls=%async_computation.19 | async-start | bytes 3932160 | tf_op jit(solution)/shard_map/all_gather | solution.py:268
  62.2 204.8 %all-gather.20.cloned.1.call-start = ((), (), s32[]{:S(2)}) async-start(), calls=%async_computation.14 | async-start | bytes 3932160 | tf_op jit(solution)/shard_map/all_gather | solution.py:268
  65.2 362.0 %all-gather.22.cloned.1.call-start = ((), (), s32[]{:S(2)}) async-start(), calls=%async_computation.15 | async-start | bytes 1327104 | tf_op jit(solution)/shard_map/all_gather | solution.py:233
  65.9 422.2 %all-gather.24.cloned.1.call-start = ((), (), s32[]{:S(2)}) async-start(), calls=%async_computation.16 | async-start | bytes 5308416 | tf_op jit(solution)/shard_map/all_gather | solution.py:234
  66.7 429.8 %all-gather.26.cloned.1.call-start = ((), (), s32[]{:S(2)}) async-start(), calls=%async_computation.17 | async-start | bytes 5308416 | tf_op jit(solution)/shard_map/all_gather | solution.py:235
  67.3 838.9 %reduce-scatter.19.cloned.1.call-start = ((), (), s32[]{:S(2)}) async-start(), calls=%async_computation.21 | async-start | bytes 7864320 | tf_op jit(solution)/shard_map/reduce_scatter | solution.py:345
  89.1 212.9 %copy-start = (bf16[512,768]{0,1:T(8,128)(2,1)}, bf16[512,768]{0,1:T(8,128)(2,1)S(1)}, u32[]{:S(2)}) copy-start(bf16[512,768]{0,1:T(8,128)(2,1)S(1)} %copy.203) | copy-start | bytes 2359300
  93.8 253.3 %copy-start.2 = (bf16[512,768]{0,1:T(8,128)(2,1)}, bf16[512,768]{0,1:T(8,128)(2,1)S(1)}, u32[]{:S(2)}) copy-start(bf16[512,768]{0,1:T(8,128)(2,1)S(1)} %copy.190) | copy-start | bytes 2359300
  574.7 335.0 %reduce-scatter.23.cloned.1.call-start = ((), (), s32[]{:S(2)}) async-start(), calls=%async_computation.23 | async-start | bytes 7864320 | tf_op jit(solution)/shard_map/reduce_scatter | solution.py:345
  628.5 289.1 %reduce-scatter.17.cloned.1.call-start = ((), (), s32[]{:S(2)}) async-start(), calls=%async_computation.20 | async-start | bytes 7864320 | tf_op jit(solution)/shard_map/reduce_scatter | solution.py:339
  753.5 180.9 %reduce-scatter.21.cloned.1.call-start = ((), (), s32[]{:S(2)}) async-start(), calls=%async_computation.22 | async-start | bytes 7864320 | tf_op jit(solution)/shard_map/reduce_scatter | solution.py:339
  864.0 117.3 %reduce-scatter.25.cloned.1.call-start = ((), (), s32[]{:S(2)}) async-start(), calls=%async_computation.24 | async-start | bytes 2654208 | tf_op jit(solution)/shard_map/reduce_scatter | solution.py:380
  868.4 142.1 %reduce-scatter.31.cloned.1.call-start = ((), (), s32[]{:S(2)}) async-start(), calls=%async_computation.27 | async-start | bytes 2654208
  906.1 142.1 %reduce-scatter.35.cloned.1.call-start = ((), (), s32[]{:S(2)}) async-start(), calls=%async_computation.29 | async-start | bytes 2654208
  917.5 168.2 %reduce-scatter.33.cloned.1.call-start = ((), (), s32[]{:S(2)}) async-start(), calls=%async_computation.28 | async-start | bytes 2654208
  941.9 244.9 %reduce-scatter.29.cloned.1.call-start = ((), (), s32[]{:S(2)}) async-start(), calls=%async_computation.26 | async-start | bytes 10616832 | tf_op jit(solution)/shard_map/reduce_scatter | solution.py:380
  958.4 328.4 %reduce-scatter.27.cloned.1.call-start = ((), (), s32[]{:S(2)}) async-start(), calls=%async_computation.25 | async-start | bytes 10616832 | tf_op jit(solution)/shard_map/reduce_scatter | solution.py:380
  970.9 387.3 %all-reduce.23.cloned.1.call-start = ((), (), s32[]{:S(2)}) async-start(), calls=%async_computation.30 | async-start | bytes 3833856 | tf_op jit(solution)/shard_map/psum | solution.py:381
  981.3 307.7 %copy-start.8 = (f32[512,768]{0,1:T(8,128)S(1)}, f32[512,768]{0,1:T(8,128)}, u32[]{:S(2)}) copy-start(f32[512,768]{0,1:T(8,128)} %reduce-scatter.23.cloned.1.call-done) | copy-start | bytes 4718596
  (131 other events, 1525.4 us)
Sparse Core Ops, SparseCore 0:
  9.7 25.5 all-gather.11
  36.9 22.3 all-gather.17
  60.9 22.3 all-gather.15
  85.5 43.6 all-gather.27
  131.4 43.9 all-gather.13
  177.2 43.9 all-gather.29
  223.0 43.9 all-gather.19
  268.7 22.6 all-gather.21
  293.0 51.4 all-gather.23
  346.0 50.5 all-gather.25
  574.8 70.3 reduce-scatter.18
  648.1 70.1 reduce-scatter.22
  753.6 70.1 reduce-scatter.16
  864.1 70.2 reduce-scatter.20
  936.5 36.3 reduce-scatter.24
  975.1 35.3 reduce-scatter.30
  1012.6 35.4 reduce-scatter.34
  1050.3 35.3 reduce-scatter.32
  1088.1 98.6 reduce-scatter.28
  1188.9 97.8 reduce-scatter.26
  1291.3 66.8 all-reduce.22
where the time goes:
time: 1380 us
  waiting for transfers between devices  472 us (34%)
  matrix products  385 us (28%)
  other arithmetic  327 us (24%)
  local copies, waits for them, and re-layouts  93.1 us (7%)
  blocking collectives  79.7 us (6%)
  between operations  19 us (1%)
    reduce_scatter x3, waiting for transfers between devices, local(): summed = lax.psum_scatter(totals, 'shard', scatter_dimension=0, tiled=True)  197 us
    sub x2, other arithmetic, attend_backward(): grad_scores = (chances * (grad_chances - centre)).astype(jnp.bfloat16)  164 us
    unnamed x24, waiting for transfers between devices  103 us
    convert_element_type x2, other arithmetic, attend_backward(): chance_low = chances.astype(jnp.bfloat16)  78.5 us
    all_gather x2, waiting for transfers between devices, local(): lax.all_gather(values_local, 'rep', axis=0, tiled=True)  75.8 us
    all_gather x2, waiting for transfers between devices, local(): lax.all_gather(keys_local, 'rep', axis=0, tiled=True)  58.8 us
    unnamed x2, blocking collectives  57 us
    dot_general x8, matrix products, block_scores(): unmasked = product()  56.7 us
  transfers between devices with their start and end apart: 21, of which 12 were waited for; matrix products, arithmetic and copies ran while one was open for 51% of the time, Pallas kernels for 0%

commit v1 on v0

--- a/solution.py
+++ b/solution.py
@@ -7,6 +7,19 @@
 HEAD_DIM = 64
 masked_value = -1e30
 norm_eps = 1e-05
+
+
+def gather_around(x, axis, dim):
+    length, place, rows = (lax.axis_size(axis), lax.axis_index(axis), x.shape[dim])
+    forward = [(i, (i + 1) % length) for i in range(length)]
+    whole = jnp.zeros((*x.shape[:dim], length * rows, *x.shape[dim + 1 :]), x.dtype)
+    held = x
+    for step in range(length):
+        holder = (place - step) % length
+        whole = lax.dynamic_update_slice_in_dim(whole, held, holder * rows, axis=dim)
+        if step < length - 1:
+            held = lax.ppermute(held, axis, forward)
+    return whole
 
 
 def as_sent(array):
@@ -266,7 +279,7 @@
         values_local = (dense(inputs_now, value_matrix) + value_vector).astype(jnp.bfloat16)
         keys_whole, values_whole = (
             lax.all_gather(keys_local, "rep", axis=0, tiled=True),
-            lax.all_gather(values_local, "rep", axis=0, tiled=True),
+            gather_around(values_local, "rep", 0),
         )
         mixture, logsums = attend_forward(
             heads_of(queries),

time: 1380 us -> 1370 us (level)
  waiting for transfers between devices: 472 us -> 441 us
    ppermute x0 -> x6, waiting for transfers between devices: none -> 84.6 us  [gather_around(): held = lax.ppermute(held, axis, forward)]
    all_gather x2 -> x0, waiting for transfers between devices: 75.8 us -> none  [local(): lax.all_gather(values_local, 'rep', axis=0, tiled=True)]
    all_gather x2, waiting for transfers between devices: 58.8 us -> 0.01 us  [local(): lax.all_gather(keys_local, 'rep', axis=0, tiled=True)]
    all_gather x1, waiting for transfers between devices: 5.35 us -> 25.5 us  [local(): lax.all_gather(shards[1], 'shard', axis=0, tiled=True)]
    slice x10 -> x2, local copies, waits for them, and re-layouts: 25.7 us -> 7.32 us  [attend_forward(): value_block = value_heads[number * block_rows:(number + 1) * block_rows]]
    dynamic_update_slice x0 -> x7, local copies, waits for them, and re-layouts: none -> 14.3 us  [gather_around(): lax.dynamic_update_slice_in_dim(whole, held, holder * rows, axis=dim)]
    unnamed x304 -> x322, local copies, waits for them, and re-layouts: 39.3 us -> 33.3 us
    unnamed x24 -> x22, waiting for transfers between devices: 103 us -> 103 us
  transfers between devices with their start and end apart: 21 -> 25, of which waited for: 12 -> 13; matrix products, arithmetic and copies ran while one was open for 51% -> 52% of each run, Pallas kernels for 0% -> 0%
where the time goes in v1:
time: 1370 us; the launch traced here: 1360 us
  waiting for transfers between devices  441 us (32%)
  matrix products  384 us (28%)
  other arithmetic  326 us (24%)
  local copies, waits for them, and re-layouts  103 us (8%)
  blocking collectives  77 us (6%)
  between operations  18.9 us (1%)
    reduce_scatter x3, waiting for transfers between devices, local(): summed = lax.psum_scatter(totals, 'shard', scatter_dimension=0, tiled=True)  197 us
    sub x2, other arithmetic, attend_backward(): grad_scores = (chances * (grad_chances - centre)).astype(jnp.bfloat16)  164 us
    unnamed x22, waiting for transfers between devices  103 us
    ppermute x6, waiting for transfers between devices, gather_around(): held = lax.ppermute(held, axis, forward)  84.6 us
    convert_element_type x2, other arithmetic, attend_backward(): chance_low = chances.astype(jnp.bfloat16)  78.4 us
    dot_general x8, matrix products, block_scores(): unmasked = product()  55.9 us
    unnamed x2, blocking collectives  54.3 us
    dot_general x8, matrix products, attend_backward(): pieces.append(product())  51.3 us
  transfers between devices with their start and end apart: 25, of which 13 were waited for; matrix products, arithmetic and copies ran while one was open for 52% of the time, Pallas kernels for 0%

profile of v1, /device:TPU:0, one launch (start us, length us, event | category | flops | bytes accessed | tf_op | source)
XLA Modules:
  0.0 1360.1 jit_solution(6395063207070383596)
XLA Ops:
  9.6 25.5 %all-gather.14.cloned.1.call-done = bf16[768,768]{1,0:T(8,128)(2,1)} async-done(((bf16[96,768]{1,0:T(8,128)(2,1)}), bf16[768,768]{1,0:T(8,128)(2,1)}) %all-gather.14.cloned.1.call-update) | async-done | bytes 1179664 | tf_op jit(solution)/shard_map/all_gather | solution.py:244
  46.6 27.9 %all-reduce.18 = (bf16[768]{0:T(1024)(128)(2,1)S(1)}, bf16[768]{0:T(1024)(128)(2,1)S(1)}, bf16[768]{0:T(1024)(128)(2,1)S(1)}, bf16[768]{0:T(1024)(128)(2,1)S(1)}...) all-reduce(bf16[768]{0:T(1024)(128)(2,1)S(1)} %dynamic-update-slice, ...), channel_id=1, replica_groups=mesh['rep'=4,'shard'=8] {'shard'}, use_global_device_ids=true, to_apply=%add | all-reduce | flops 6144 | bytes 24576
  84.8 12.7 all-gather
  101.8 24.1 %collective-permute-done.3 = bf16[512,768]{1,0:T(8,128)(2,1)} collective-permute-done((bf16[512,768]{1,0:T(8,128)(2,1)S(1)}, bf16[512,768]{1,0:T(8,128)(2,1)}, u32[]{:S(2)}, u32[]{:S(2)}) %collective-permute-start.3) | collective-permute-done | bytes 786464 | tf_op jit(solution)/shard_map/ppermute | solution.py:21
  138.4 18.7 %collective-permute-done.1 = bf16[512,768]{1,0:T(8,128)(2,1)} collective-permute-done((bf16[512,768]{1,0:T(8,128)(2,1)}, bf16[512,768]{1,0:T(8,128)(2,1)}, u32[]{:S(2)}, u32[]{:S(2)}) %collective-permute-start.1) | collective-permute-done | bytes 786464 | tf_op jit(solution)/shard_map/ppermute | solution.py:21
  157.7 23.1 %collective-permute-done.4 = bf16[512,768]{1,0:T(8,128)(2,1)} collective-permute-done((bf16[512,768]{1,0:T(8,128)(2,1)}, bf16[512,768]{1,0:T(8,128)(2,1)}, u32[]{:S(2)}, u32[]{:S(2)}) %collective-permute-start.4) | collective-permute-done | bytes 786464 | tf_op jit(solution)/shard_map/ppermute | solution.py:21
  210.2 18.2 %collective-permute-done.5 = bf16[512,768]{1,0:T(8,128)(2,1)} collective-permute-done((bf16[512,768]{1,0:T(8,128)(2,1)}, bf16[512,768]{1,0:T(8,128)(2,1)}, u32[]{:S(2)}, u32[]{:S(2)}) %collective-permute-start.5) | collective-permute-done | bytes 786464 | tf_op jit(solution)/shard_map/ppermute | solution.py:21
  294.8 17.6 %fusion.5 = f32[12,512]{1,0:T(8,128)S(1)} fusion(f32[12,512]{1,0:T(8,128)S(1)} %maximum_maximum_fusion, f32[12,512,512]{1,2,0:T(8,128)} %get-tuple-element.199, f32[12,512,512]{1,2,0:T(8,128)} %get-tuple-element.201, f32[12,512,512]{1,2,0:T(8,128)} %get-tuple-element.205, f32[12,512,512]{1,2,0:T(8,128)} %get-tuple-element.203), kind=kLoop, calls=%fused_computation.19 | loop fusion | flops 62908416 | bytes 50380800 | tf_op jit(solution)/shard_map/reduce_sum | solution.py:91
  340.1 17.2 %fusion.4 = f32[12,512]{1,0:T(8,128)S(1)} fusion(f32[12,512]{1,0:T(8,128)S(1)} %maximum_maximum_fusion.1, f32[12,512,512]{1,2,0:T(8,128)} %get-tuple-element.187, f32[12,512,512]{1,2,0:T(8,128)} %get-tuple-element.189, f32[12,512,512]{1,2,0:T(8,128)} %get-tuple-element.193, f32[12,512,512]{1,2,0:T(8,128)} %get-tuple-element.191), kind=kLoop, calls=%fused_computation.18 | loop fusion | flops 62908416 | bytes 50380800 | tf_op jit(solution)/shard_map/reduce_sum | solution.py:91
  357.4 39.3 %fusion.6 = (bf16[12,512,2048]{1,2,0:T(8,128)(2,1)}, bf16[12,512,2048]{1,2,0:T(8,128)(2,1)}) fusion(f32[12,512]{1,0:T(8,128)S(1)} %log_add_fusion.1, f32[12,512,512]{1,2,0:T(8,128)} %get-tuple-element.187, f32[12,512,512]{1,2,0:T(8,128)} %get-tuple-element.189, f32[12,512,512]{1,2,0:T(8,128)} %get-tuple-element.193, f32[12,512,512]{1,2,0:T(8,128)} %get-tuple-element.191, ...), kind=kLoop, calls=%fused_computation.20 | loop fusion | flops 100663296 | bytes 100737024 | tf_op jit(solution)/shard_map/convert_element_type | solution.py:129
  416.9 39.2 %fusion.9 = (bf16[12,512,2048]{1,2,0:T(8,128)(2,1)}, bf16[12,512,2048]{1,2,0:T(8,128)(2,1)}) fusion(f32[12,512]{1,0:T(8,128)S(1)} %log_add_fusion, f32[12,512,512]{1,2,0:T(8,128)} %get-tuple-element.199, f32[12,512,512]{1,2,0:T(8,128)} %get-tuple-element.201, f32[12,512,512]{1,2,0:T(8,128)} %get-tuple-element.205, f32[12,512,512]{1,2,0:T(8,128)} %get-tuple-element.203, ...), kind=kLoop, calls=%fused_computation.21 | loop fusion | flops 100663296 | bytes 100737024 | tf_op jit(solution)/shard_map/convert_element_type | solution.py:129
  508.5 18.1 %convert_reduce_fusion.1 = (f32[3072]{0:T(1024)}, bf16[512,3072]{1,0:T(8,128)(2,1)}, f32[3072]{0:T(1024)}, bf16[512,3072]{1,0:T(8,128)(2,1)S(1)}) fusion(f32[512,3072]{1,0:T(8,128)} %fusion.190, f32[3072]{0:T(1024)S(1)} %bitcast.362, f32[512,3072]{1,0:T(8,128)} %fusion.223, f32[512,3072]{1,0:T(8,128)} %copy-done.133, ...), kind=kOutput, calls=%fused_computation.87 | convolution fusion | flops 2488264704 | bytes 30707712 | tf_op jit(solution)/shard_map/dot_general | solution.py:46
  614.8 76.6 %multiply_convert_fusion.1 = bf16[12,512,2048]{1,2,0:T(8,128)(2,1)} fusion(f32[12,512,512]{1,2,0:T(8,128)} %fusion.221, f32[12,512,512]{1,2,0:T(8,128)} %fusion.220, f32[12,512,512]{1,2,0:T(8,128)} %fusion.219, f32[12,512,512]{1,2,0:T(8,128)} %fusion.218, f32[12,512]{1,0:T(8,128)S(1)} %copy-done.86, f32[12,512,512]{1,2,0:T(8,128)} %get-tuple-element.187, ...), kind=kOutput, calls=%fused_computation.10 | output fusion | flops 226500608 | bytes 125853696 | tf_op jit(solution)/shard_map/sub | solution.py:140
  740.3 87.0 %multiply_convert_fusion = bf16[12,512,2048]{1,2,0:T(8,128)(2,1)} fusion(f32[12,512,512]{1,2,0:T(8,128)} %fusion.227, f32[12,512,512]{1,2,0:T(8,128)} %fusion.226, f32[12,512,512]{1,2,0:T(8,128)} %fusion.225, f32[12,512,512]{1,2,0:T(8,128)} %fusion.224, f32[12,512]{1,0:T(8,128)S(1)} %copy-done.84, f32[12,512,512]{1,2,0:T(8,128)} %get-tuple-element.199, ...), kind=kOutput, calls=%fused_computation.6 | output fusion | flops 226500608 | bytes 125853696 | tf_op jit(solution)/shard_map/sub | solution.py:140
  905.6 12.4 reduce-scatter.21.cloned.1.call-done
  931.8 10.2 convolution_add_fusion
  966.6 27.6 %reduce-scatter.31.cloned.1.call-done = f32[96,768]{1,0:T(8,128)} async-done(((f32[768,768]{1,0:T(8,128)}), f32[96,768]{1,0:T(8,128)}) %reduce-scatter.31.cloned.1.call-update) | async-done | bytes 294928
  996.2 35.7 %reduce-scatter.35.cloned.1.call-done = f32[96,768]{1,0:T(8,128)} async-done(((f32[768,768]{1,0:T(8,128)}), f32[96,768]{1,0:T(8,128)}) %reduce-scatter.35.cloned.1.call-update) | async-done | bytes 294928
  1033.7 35.9 %reduce-scatter.33.cloned.1.call-done = f32[96,768]{1,0:T(8,128)} async-done(((f32[768,768]{1,0:T(8,128)}), f32[96,768]{1,0:T(8,128)}) %reduce-scatter.33.cloned.1.call-update) | async-done | bytes 294928
  1071.4 99.1 %reduce-scatter.29.cloned.1.call-done = f32[384,768]{1,0:T(8,128)} async-done(((f32[3072,768]{1,0:T(8,128)}), f32[384,768]{1,0:T(8,128)}) %reduce-scatter.29.cloned.1.call-update) | async-done | bytes 1179664 | tf_op jit(solution)/shard_map/reduce_scatter | solution.py:393
  1172.6 97.9 %reduce-scatter.27.cloned.1.call-done = f32[96,3072]{1,0:T(8,128)} async-done(((f32[768,3072]{1,0:T(8,128)}), f32[96,3072]{1,0:T(8,128)}) %reduce-scatter.27.cloned.1.call-update) | async-done | bytes 1179664 | tf_op jit(solution)/shard_map/reduce_scatter | solution.py:393
  1272.9 26.4 %all-reduce.17 = (bf16[768]{0:T(1024)(128)(2,1)S(1)}, bf16[768]{0:T(1024)(128)(2,1)S(1)}, bf16[768]{0:T(1024)(128)(2,1)S(1)}, bf16[3072]{0:T(1024)(128)(2,1)S(1)...) all-reduce(f32[768]{0:T(1024)S(1)} %add.489, ...), channel_id=12, replica_groups=mesh['rep'=4,'shard'=8] {'shard'}, use_global_device_ids=true, to_apply=%region_46.47.clone | all-reduce | flops 9216 | bytes 55296
  1300.1 10.0 all-reduce.19
  1323.8 18.0 %all-reduce.23.cloned.1.call-done = (bf16[96,768]{0,1:T(8,128)(2,1)}, bf16[96,768]{0,1:T(8,128)(2,1)}, bf16[96,768]{0,1:T(8,128)(2,1)}, bf16[96,768]{1,0:T(8,128...) async-done(((bf16[96,768]{0,1:T(8,128)(2,1)}, bf16[96,768]{0,1:T(8,128)(2,1)}, bf16[96,768]{0,1:T(8,128)(2,1)}, bf16[96,768]{1,0:T(8,128)(2,1)}, ...) | async-done | bytes 1769488 | tf_op jit(solution)/shard_map/psum | solution.py:394
  (575 shorter events, 522.8 us)
Async XLA Ops:
  7.2 27.9 %all-gather.14.cloned.1.call-start = ((), (), s32[]{:S(2)}) async-start(), calls=%async_computation.12 | async-start | bytes 1327104 | tf_op jit(solution)/shard_map/all_gather | solution.py:244
  7.9 66.6 %all-gather.10.cloned.1.call-start = ((), (), s32[]{:S(2)}) async-start(), calls=%async_computation.10 | async-start | bytes 1327104 | tf_op jit(solution)/shard_map/all_gather | solution.py:245
  8.7 122.8 %all-gather.12.cloned.1.call-start = ((), (), s32[]{:S(2)}) async-start(), calls=%async_computation.11 | async-start | bytes 1327104 | tf_op jit(solution)/shard_map/all_gather | solution.py:243
  9.5 231.1 %all-gather.24.cloned.1.call-start = ((), (), s32[]{:S(2)}) async-start(), calls=%async_computation.17 | async-start | bytes 3932160 | tf_op jit(solution)/shard_map/all_gather | solution.py:281
  38.3 215.2 %all-gather.16.cloned.1.call-start = ((), (), s32[]{:S(2)}) async-start(), calls=%async_computation.13 | async-start | bytes 3932160 | tf_op jit(solution)/shard_map/all_gather | solution.py:281
  41.3 371.6 %all-gather.18.cloned.1.call-start = ((), (), s32[]{:S(2)}) async-start(), calls=%async_computation.14 | async-start | bytes 1327104 | tf_op jit(solution)/shard_map/all_gather | solution.py:246
  41.9 431.9 %all-gather.20.cloned.1.call-start = ((), (), s32[]{:S(2)}) async-start(), calls=%async_computation.15 | async-start | bytes 5308416 | tf_op jit(solution)/shard_map/all_gather | solution.py:247
  42.7 439.5 %all-gather.22.cloned.1.call-start = ((), (), s32[]{:S(2)}) async-start(), calls=%async_computation.16 | async-start | bytes 5308416 | tf_op jit(solution)/shard_map/all_gather | solution.py:248
  43.4 847.3 %reduce-scatter.19.cloned.1.call-start = ((), (), s32[]{:S(2)}) async-start(), calls=%async_computation.19 | async-start | bytes 7864320 | tf_op jit(solution)/shard_map/reduce_scatter | solution.py:358
  80.2 45.7 %collective-permute-start.3 = (bf16[512,768]{1,0:T(8,128)(2,1)S(1)}, bf16[512,768]{1,0:T(8,128)(2,1)}, u32[]{:S(2)}, u32[]{:S(2)}) collective-permute-start(bf16[512,768]{1,0:T(8,128)(2,1)S(1)} %add_convert_fusion.5), channel_id=1, source_target_pairs={{0,8},{8,16},{16,24},{24,0},{1,9},{9,17},{17,25},{25,1},{2,10},{10... | collective-permute-start | bytes 2359304 | tf_op jit(solution)/shard_map/ppermute | solution.py:21
  100.0 57.1 %collective-permute-start.1 = (bf16[512,768]{1,0:T(8,128)(2,1)}, bf16[512,768]{1,0:T(8,128)(2,1)}, u32[]{:S(2)}, u32[]{:S(2)}) collective-permute-start(bf16[512,768]{1,0:T(8,128)(2,1)} %collective-permute-done), channel_id=1, source_target_pairs={{0,8},{8,16},{16,24},{24,0},{1,9},{9,17},{17,25},{25,1},{2,10},{10... | collective-permute-start | bytes 2359304 | tf_op jit(solution)/shard_map/ppermute | solution.py:21
  125.9 54.9 %collective-permute-start.4 = (bf16[512,768]{1,0:T(8,128)(2,1)}, bf16[512,768]{1,0:T(8,128)(2,1)}, u32[]{:S(2)}, u32[]{:S(2)}) collective-permute-start(bf16[512,768]{1,0:T(8,128)(2,1)} %collective-permute-done.3), channel_id=1, source_target_pairs={{0,8},{8,16},{16,24},{24,0},{1,9},{9,17},{17,25},{25,1},{2,10},{10... | collective-permute-start | bytes 2359304 | tf_op jit(solution)/shard_map/ppermute | solution.py:21
  157.1 50.7 %collective-permute-start.2 = (bf16[512,768]{1,0:T(8,128)(2,1)}, bf16[512,768]{1,0:T(8,128)(2,1)}, u32[]{:S(2)}, u32[]{:S(2)}) collective-permute-start(bf16[512,768]{1,0:T(8,128)(2,1)} %collective-permute-done.1), channel_id=1, source_target_pairs={{0,8},{8,16},{16,24},{24,0},{1,9},{9,17},{17,25},{25,1},{2,10},{10... | collective-permute-start | bytes 2359304 | tf_op jit(solution)/shard_map/ppermute | solution.py:21
  180.8 47.5 %collective-permute-start.5 = (bf16[512,768]{1,0:T(8,128)(2,1)}, bf16[512,768]{1,0:T(8,128)(2,1)}, u32[]{:S(2)}, u32[]{:S(2)}) collective-permute-start(bf16[512,768]{1,0:T(8,128)(2,1)} %collective-permute-done.4), channel_id=1, source_target_pairs={{0,8},{8,16},{16,24},{24,0},{1,9},{9,17},{17,25},{25,1},{2,10},{10... | collective-permute-start | bytes 2359304 | tf_op jit(solution)/shard_map/ppermute | solution.py:21
  560.3 334.1 %reduce-scatter.23.cloned.1.call-start = ((), (), s32[]{:S(2)}) async-start(), calls=%async_computation.21 | async-start | bytes 7864320 | tf_op jit(solution)/shard_map/reduce_scatter | solution.py:358
  614.1 287.8 %reduce-scatter.17.cloned.1.call-start = ((), (), s32[]{:S(2)}) async-start(), calls=%async_computation.18 | async-start | bytes 7864320 | tf_op jit(solution)/shard_map/reduce_scatter | solution.py:352
  739.5 178.5 %reduce-scatter.21.cloned.1.call-start = ((), (), s32[]{:S(2)}) async-start(), calls=%async_computation.20 | async-start | bytes 7864320 | tf_op jit(solution)/shard_map/reduce_scatter | solution.py:352
  849.4 115.4 %reduce-scatter.25.cloned.1.call-start = ((), (), s32[]{:S(2)}) async-start(), calls=%async_computation.22 | async-start | bytes 2654208 | tf_op jit(solution)/shard_map/reduce_scatter | solution.py:393
  853.8 140.4 %reduce-scatter.31.cloned.1.call-start = ((), (), s32[]{:S(2)}) async-start(), calls=%async_computation.25 | async-start | bytes 2654208
  890.7 141.2 %reduce-scatter.35.cloned.1.call-start = ((), (), s32[]{:S(2)}) async-start(), calls=%async_computation.27 | async-start | bytes 2654208
  901.9 167.8 %reduce-scatter.33.cloned.1.call-start = ((), (), s32[]{:S(2)}) async-start(), calls=%async_computation.26 | async-start | bytes 2654208
  925.5 245.0 %reduce-scatter.29.cloned.1.call-start = ((), (), s32[]{:S(2)}) async-start(), calls=%async_computation.24 | async-start | bytes 10616832 | tf_op jit(solution)/shard_map/reduce_scatter | solution.py:393
  942.1 328.4 %reduce-scatter.27.cloned.1.call-start = ((), (), s32[]{:S(2)}) async-start(), calls=%async_computation.23 | async-start | bytes 10616832 | tf_op jit(solution)/shard_map/reduce_scatter | solution.py:393
  954.4 387.4 %all-reduce.23.cloned.1.call-start = ((), (), s32[]{:S(2)}) async-start(), calls=%async_computation.28 | async-start | bytes 3833856 | tf_op jit(solution)/shard_map/psum | solution.py:394
  (144 other events, 2607.3 us)
Sparse Core Ops, SparseCore 0:
  9.7 25.3 all-gather.13
  36.7 22.5 all-gather.9
  61.0 22.3 all-gather.11
  85.0 69.7 all-gather.23
  156.6 68.2 all-gather.15
  226.3 22.6 all-gather.17
  250.7 51.4 all-gather.19
  303.8 50.5 all-gather.21
  560.5 68.4 reduce-scatter.18
  631.8 70.1 reduce-scatter.22
  739.6 67.8 reduce-scatter.16
  849.6 68.3 reduce-scatter.20
  920.3 36.1 reduce-scatter.24
  958.7 35.4 reduce-scatter.30
  996.4 35.4 reduce-scatter.34
  1034.1 35.5 reduce-scatter.32
  1071.8 98.6 reduce-scatter.28
  1172.6 97.8 reduce-scatter.26
  1275.0 66.8 all-reduce.22
